TPU v7x, 32 devices: a whole 2x2x4 slice. The times are simulated.
32 devices in a mesh: row: 8 (over z, core), col: 4 (over y, x).
Axes of the slice: x: 2, y: 2, z: 4, core: 2. Of those that a mesh axis runs over, the one named last changes fastest.
Arguments:
- points: bfloat16 [2048, 1024], P(('row', 'col')), may hold values from -6 to 6
- factor: float32 [2048, 256], P(('row', 'col')), may hold values from 0 to 1
Outputs:
- factor_out: float32 [2048, 256], P(('row', 'col'))
All inputs are finite; a program needn't handle non-finite values.
Results may differ from a plain program's by a relative error of at most 0.002.
The roundings to bfloat16 on the way count: a program that leaves them out, or rounds other values in their place, can miss the bound.
Values may be sent and summed in bfloat16 or wider, within the bound.
A program may use at most 64 MiB of HBM per device.

v0:
```python
import math
import jax
import jax.numpy as jnp
from jax import lax
from jax.sharding import PartitionSpec as P

EMBED_WIDTH = 1024
ITERS = 2


def shards(points, factor):
    nrow = lax.axis_size("row")
    ncol = lax.axis_size("col")
    pts = points.shape[0]
    rank = factor.shape[1]
    total = pts * nrow * ncol
    row_pts = lax.all_gather(points, "col", axis=0, tiled=True)
    col_pts = lax.all_gather(points, "row", axis=0, tiled=True)
    gram_matrix = lax.dot_general(
        row_pts, col_pts, (((1,), (1,)), ((), ())), preferred_element_type=jnp.float32
    )
    row_sq = jnp.sum(jnp.square(row_pts.astype(jnp.float32)), axis=1)
    col_sq = jnp.sum(jnp.square(col_pts.astype(jnp.float32)), axis=1)
    kern = jnp.exp((2.0 * gram_matrix - row_sq[:, None] - col_sq[None, :]) * (0.5 / EMBED_WIDTH))
    row_sum, band = lax.psum((jnp.sum(kern, axis=1), jnp.sum(kern)), "col")
    col_sum, grand = lax.psum((jnp.sum(kern, axis=0), band), "row")
    affinity = (
        kern - row_sum[:, None] / total - col_sum[None, :] / total + grand / (total * total)
    ).astype(jnp.bfloat16)
    unit = 2.0 / math.sqrt(total * rank)
    h = factor * unit
    for step in range(ITERS):
        hb = h.astype(jnp.bfloat16)
        copies = lax.all_gather(hb, "row", axis=0, tiled=True)
        ah = lax.psum_scatter(
            jnp.dot(affinity, copies, preferred_element_type=jnp.float32),
            "col",
            scatter_dimension=0,
            tiled=True,
        )
        local_gram = lax.dot_general(
            h, h, (((0,), (0,)), ((), ())), precision=lax.Precision.HIGHEST
        )
        hh = lax.psum(local_gram, ("row", "col"))
        scale = 0.5 / jnp.sqrt(jnp.sum(hh * hh) + 1e-06)
        h = jnp.maximum(h - scale * (jnp.dot(h, hh, precision=lax.Precision.HIGHEST) - ah), 0.0)
    return h / unit


def solution(mesh):
    in_specs = (P(("row", "col"), None), P(("row", "col"), None))
    out_specs = P(("row", "col"), None)
    return jax.shard_map(shards, mesh=mesh, in_specs=in_specs, out_specs=out_specs, check_vma=False)
```

profile of v0, /device:TPU:0, one launch (start us, length us, event | category | flops | bytes accessed | tf_op | source)
XLA Modules:
  0.0 301.0 jit_solution(7194826416192646812)
XLA Ops:
  7.4 0.0 copy-start.1
  7.4 0.0 all-gather.2.cloned.1.call-start
  7.4 0.7 all-gather.2.cloned.1.call-update
  8.1 0.0 all-reduce.5.cloned.1.call-start
  8.1 2.0 fusion.12
  10.2 0.0 all-reduce.5.cloned.1.call-update
  10.2 0.0 reduce-scatter.3.cloned.1.call-start
  10.3 11.9 %all_gather.12 = bf16[256,1024]{1,0:T(8,128)(2,1)S(1)} all-gather(bf16[64,1024]{1,0:T(8,128)(2,1)} %param.2), channel_id=1, replica_groups=mesh['row'=8,'col'=4] {'col'}, dimensions={0}, use_global_device_ids=true | all-gather | bytes 655360 | tf_op jit(solution)/shard_map/all_gather | solution.py:17
  22.1 0.0 copy-done.1
  22.2 0.2 multiply_reduce_fusion.1
  22.3 15.2 %all_gather.14 = bf16[512,256]{1,0:T(8,128)(2,1)S(1)} all-gather(bf16[64,256]{1,0:T(8,128)(2,1)S(1)} %multiply_convert_fusion), channel_id=1, replica_groups=mesh['row'=8,'col'=4] {'row'}, dimensions={0}, use_global_device_ids=true | all-gather | bytes 294912 | tf_op jit(solution)/shard_map/all_gather | solution.py:34
  37.6 0.0 all-gather.2.cloned.1.call-done
  37.6 0.0 copy-start
  37.6 1.6 multiply_reduce_fusion
  39.2 0.0 copy-done
  39.2 1.2 fusion.20
  40.4 9.6 %all-reduce.1 = (f32[]{:T(128)}, f32[256]{0:T(256)S(1)}) all-reduce(f32[]{:T(128)} %get-tuple-element.6, f32[256]{0:T(256)S(1)} %get-tuple-element.5), channel_id=1, replica_groups=mesh['row'=8,'col'=4] {'col'}, use_global_device_ids=true, to_apply=%region_9.0 | all-reduce | flops 257 | bytes 2056 | tf_op jit(solution)/shard_map/psum | solution.py:25
  50.0 15.4 %all-reduce = (f32[]{:T(128)}, f32[512]{0:T(512)S(1)}) all-reduce(f32[]{:T(128)} %get-tuple-element.10, f32[512]{0:T(512)S(1)} %get-tuple-element.7), channel_id=1, replica_groups=mesh['row'=8,'col'=4] {'row'}, use_global_device_ids=true, to_apply=%region_10.0 | all-reduce | flops 513 | bytes 4104 | tf_op jit(solution)/shard_map/psum | solution.py:26
  66.1 1.0 fusion.19
  67.1 0.0 reduce-scatter.3.cloned.1.call-update
  67.1 0.0 all-reduce.7.cloned.1.call-start
  67.2 78.5 %all-reduce.5.cloned.1.call-done = f32[256,256]{1,0:T(8,128)} async-done(((f32[256,256]{1,0:T(8,128)}), f32[256,256]{1,0:T(8,128)}) %all-reduce.5.cloned.1.call-update) | async-done | bytes 262160 | tf_op jit(solution)/shard_map/psum | solution.py:44
  145.6 1.6 multiply_reduce_fusion.3
  147.9 0.0 reduce-scatter.3.cloned.1.call-done
  148.0 1.2 fusion.21
  149.2 14.2 %all_gather.15 = bf16[512,256]{1,0:T(8,128)(2,1)S(1)} all-gather(bf16[64,256]{1,0:T(8,128)(2,1)S(1)} %get-tuple-element.13), channel_id=1, replica_groups=mesh['row'=8,'col'=4] {'row'}, dimensions={0}, use_global_device_ids=true | all-gather | bytes 294912 | tf_op jit(solution)/shard_map/all_gather | solution.py:34
  163.4 1.1 fusion.22
  164.5 0.0 all-reduce.7.cloned.1.call-update
  164.5 0.0 reduce-scatter.5.cloned.1.call-start
  164.6 1.0 fusion.18
  165.6 0.0 reduce-scatter.5.cloned.1.call-update
  165.6 124.1 %all-reduce.7.cloned.1.call-done = f32[256,256]{1,0:T(8,128)} async-done(((f32[256,256]{1,0:T(8,128)}), f32[256,256]{1,0:T(8,128)}) %all-reduce.7.cloned.1.call-update) | async-done | bytes 262160 | tf_op jit(solution)/shard_map/psum | solution.py:44
  289.7 1.6 multiply_reduce_fusion.2
  292.0 0.0 reduce-scatter.5.cloned.1.call-done
  292.0 1.8 fusion.7
  (3 shorter events, 0.0 us)
Async XLA Ops:
  7.4 14.8 %copy-start.1 = (f32[64,256]{1,0:T(8,128)S(1)}, f32[64,256]{1,0:T(8,128)}, u32[]{:S(2)}) copy-start(f32[64,256]{1,0:T(8,128)} %param.3) | copy-start | bytes 196612
  7.4 30.2 %all-gather.2.cloned.1.call-start = ((), (), s32[]{:S(2)}) async-start(), calls=%async_computation.3 | async-start | bytes 1179648 | tf_op jit(solution)/shard_map/all_gather | solution.py:18
  8.1 137.5 %all-reduce.5.cloned.1.call-start = ((), (), s32[]{:S(2)}) async-start(), calls=%async_computation.2 | async-start | bytes 524288 | tf_op jit(solution)/shard_map/psum | solution.py:44
  10.2 137.8 %reduce-scatter.3.cloned.1.call-start = ((), (), s32[]{:S(2)}) async-start(), calls=%async_computation.4 | async-start | bytes 327680 | tf_op jit(solution)/shard_map/reduce_scatter | solution.py:35
  37.6 1.6 copy-start
  67.1 222.6 %all-reduce.7.cloned.1.call-start = ((), (), s32[]{:S(2)}) async-start(), calls=%async_computation.5 | async-start | bytes 524288 | tf_op jit(solution)/shard_map/psum | solution.py:44
  164.5 127.5 %reduce-scatter.5.cloned.1.call-start = ((), (), s32[]{:S(2)}) async-start(), calls=%async_computation.6 | async-start | bytes 327680 | tf_op jit(solution)/shard_map/reduce_scatter | solution.py:35
Sparse Core Ops, SparseCore 0:
  9.8 26.2 all-gather.1
  67.2 21.1 reduce-scatter.2
  168.1 23.4 reduce-scatter.4
Sparse Core Ops, SparseCore 1:
  14.1 131.5 all-reduce.4
  164.6 125.0 all-reduce.6
where the time goes:
time: 301 us
  waiting for transfers between devices  203 us (67%)
  blocking collectives  66.4 us (22%)
  between operations  16.6 us (6%)
  matrix products  9.4 us (3%)
  other arithmetic  5.03 us (2%)
    psum x2, waiting for transfers between devices, shards(): hh = lax.psum(local_gram, ('row', 'col'))  203 us
    all_gather x2, blocking collectives, shards(): copies = lax.all_gather(hb, 'row', axis=0, tiled=True)  29.4 us
    psum x1, blocking collectives, shards(): col_sum, grand = lax.psum((jnp.sum(kern, axis=0), band), 'row')  15.4 us
    all_gather x1, blocking collectives, shards(): row_pts = lax.all_gather(points, 'col', axis=0, tiled=True)  11.9 us
    psum x1, blocking collectives, shards(): row_sum, band = lax.psum((jnp.sum(kern, axis=1), jnp.sum(kern)), 'col')  9.6 us
  transfers between devices with their start and end apart: 5, of which 2 were waited for; matrix products, arithmetic and copies ran while one was open for 3% of the time, Pallas kernels for 0%

commit v1 on v0

--- a/solution.py
+++ b/solution.py
@@ -6,6 +6,16 @@
 
 EMBED_WIDTH = 1024
 ITERS = 2
+
+
+def gather_by_hops(x, mesh_axis, dim):
+    size = lax.axis_size(mesh_axis)
+    current, tiles = (x, [x])
+    for _ in range(size - 1):
+        current = lax.ppermute(current, mesh_axis, [(i, (i + 1) % size) for i in range(size)])
+        tiles.insert(0, current)
+    merged = jnp.concatenate(tiles, axis=dim)
+    return jnp.roll(merged, (lax.axis_index(mesh_axis) + 1) * x.shape[dim], axis=dim)
 
 
 def shards(points, factor):
@@ -31,7 +41,7 @@
     h = factor * unit
     for step in range(ITERS):
         hb = h.astype(jnp.bfloat16)
-        copies = lax.all_gather(hb, "row", axis=0, tiled=True)
+        copies = gather_by_hops(hb, "row", 0)
         ah = lax.psum_scatter(
             jnp.dot(affinity, copies, preferred_element_type=jnp.float32),
             "col",

time: 301 us -> 336 us (1.12)
  waiting for transfers between devices: 203 us -> 267 us
  blocking collectives: 66.4 us -> 34.8 us
    ppermute x0 -> x14, waiting for transfers between devices: none -> 64.8 us  [gather_by_hops(): lax.ppermute(current, mesh_axis, [(i, (i + 1) % size) for i in range(size)])]
    all_gather x2 -> x0, blocking collectives: 29.4 us -> none  [shards(): copies = lax.all_gather(hb, 'row', axis=0, tiled=True)]
  transfers between devices with their start and end apart: 5 -> 19, of which waited for: 2 -> 15; matrix products, arithmetic and copies ran while one was open for 3% -> 4% of each run, Pallas kernels for 0% -> 0%
where the time goes in v1:
time: 336 us
  waiting for transfers between devices  267 us (79%)
  blocking collectives  34.8 us (10%)
  between operations  16.8 us (5%)
  matrix products  10.2 us (3%)
  other arithmetic  5.88 us (2%)
    psum x2, waiting for transfers between devices, shards(): hh = lax.psum(local_gram, ('row', 'col'))  202 us
    ppermute x14, waiting for transfers between devices, gather_by_hops(): lax.ppermute(current, mesh_axis, [(i, (i + 1) % size) for i in range(size)])  64.8 us
    psum x1, blocking collectives, shards(): col_sum, grand = lax.psum((jnp.sum(kern, axis=0), band), 'row')  14.2 us
    all_gather x1, blocking collectives, shards(): row_pts = lax.all_gather(points, 'col', axis=0, tiled=True)  11.1 us
    psum x1, blocking collectives, shards(): row_sum, band = lax.psum((jnp.sum(kern, axis=1), jnp.sum(kern)), 'col')  9.53 us
  transfers between devices with their start and end apart: 19, of which 15 were waited for; matrix products, arithmetic and copies ran while one was open for 4% of the time, Pallas kernels for 0%

profile of v1, /device:TPU:0, one launch (start us, length us, event | category | flops | bytes accessed | tf_op | source)
XLA Modules:
  0.0 335.8 jit_solution(8179274356328408126)
XLA Ops:
  7.4 0.0 all-gather.2.cloned.1.call-start
  7.4 0.7 all-gather.2.cloned.1.call-update
  8.1 0.0 all-reduce.5.cloned.1.call-start
  8.1 0.8 multiply_convert_fusion
  9.0 0.5 collective-permute-start
  9.5 5.6 %collective-permute-done = bf16[64,256]{1,0:T(8,128)(2,1)S(1)} collective-permute-done((bf16[64,256]{1,0:T(8,128)(2,1)S(1)}, bf16[64,256]{1,0:T(8,128)(2,1)S(1)}, u32[]{:S(2)}, u32[]{:S(2)}) %collective-permute-start) | collective-permute-done | bytes 32800 | tf_op jit(solution)/shard_map/ppermute | solution.py:15
  15.1 0.0 collective-permute-start.1
  15.1 5.1 %collective-permute-done.1 = bf16[64,256]{1,0:T(8,128)(2,1)S(1)} collective-permute-done((bf16[64,256]{1,0:T(8,128)(2,1)S(1)}, bf16[64,256]{1,0:T(8,128)(2,1)S(1)}, u32[]{:S(2)}, u32[]{:S(2)}) %collective-permute-start.1) | collective-permute-done | bytes 32800 | tf_op jit(solution)/shard_map/ppermute | solution.py:15
  20.2 0.0 collective-permute-start.2
  20.2 5.6 %collective-permute-done.2 = bf16[64,256]{1,0:T(8,128)(2,1)S(1)} collective-permute-done((bf16[64,256]{1,0:T(8,128)(2,1)S(1)}, bf16[64,256]{1,0:T(8,128)(2,1)S(1)}, u32[]{:S(2)}, u32[]{:S(2)}) %collective-permute-start.2) | collective-permute-done | bytes 32800 | tf_op jit(solution)/shard_map/ppermute | solution.py:15
  25.8 0.0 collective-permute-start.3
  25.8 5.8 %collective-permute-done.3 = bf16[64,256]{1,0:T(8,128)(2,1)S(1)} collective-permute-done((bf16[64,256]{1,0:T(8,128)(2,1)S(1)}, bf16[64,256]{1,0:T(8,128)(2,1)S(1)}, u32[]{:S(2)}, u32[]{:S(2)}) %collective-permute-start.3) | collective-permute-done | bytes 32800 | tf_op jit(solution)/shard_map/ppermute | solution.py:15
  31.6 0.0 collective-permute-start.4
  31.6 2.0 fusion.18
  33.7 0.0 copy-start
  33.7 0.0 all-reduce.5.cloned.1.call-update
  33.7 0.0 reduce-scatter.3.cloned.1.call-start
  33.7 3.0 collective-permute-done.4
  36.8 0.0 collective-permute-start.5
  36.8 11.1 %all_gather.6 = bf16[256,1024]{1,0:T(8,128)(2,1)S(1)} all-gather(bf16[64,1024]{1,0:T(8,128)(2,1)} %param.4), channel_id=1, replica_groups=mesh['row'=8,'col'=4] {'col'}, dimensions={0}, use_global_device_ids=true | all-gather | bytes 655360 | tf_op jit(solution)/shard_map/all_gather | solution.py:27
  47.8 0.0 collective-permute-done.5
  47.8 0.1 collective-permute-start.6
  47.9 0.2 multiply_reduce_fusion.1
  48.1 5.0 %collective-permute-done.6 = bf16[64,256]{1,0:T(8,128)(2,1)S(1)} collective-permute-done((bf16[64,256]{1,0:T(8,128)(2,1)S(1)}, bf16[64,256]{1,0:T(8,128)(2,1)S(1)}, u32[]{:S(2)}, u32[]{:S(2)}) %collective-permute-start.6) | collective-permute-done | bytes 32800 | tf_op jit(solution)/shard_map/ppermute | solution.py:15
  53.1 0.0 copy-done
  53.2 0.0 all-gather.2.cloned.1.call-done
  53.2 0.0 copy-start.1
  53.2 1.6 multiply_reduce_fusion
  54.8 0.0 copy-done.1
  54.8 1.2 fusion.28
  56.0 9.5 %all-reduce.1 = (f32[]{:T(128)}, f32[256]{0:T(256)S(1)}) all-reduce(f32[]{:T(128)} %get-tuple-element.7, f32[256]{0:T(256)S(1)} %get-tuple-element.6), channel_id=1, replica_groups=mesh['row'=8,'col'=4] {'col'}, use_global_device_ids=true, to_apply=%region_9.10 | all-reduce | flops 257 | bytes 2056 | tf_op jit(solution)/shard_map/psum | solution.py:35
  65.6 14.2 %all-reduce = (f32[]{:T(128)}, f32[512]{0:T(512)S(1)}) all-reduce(f32[]{:T(128)} %get-tuple-element.11, f32[512]{0:T(512)S(1)} %get-tuple-element.8), channel_id=1, replica_groups=mesh['row'=8,'col'=4] {'row'}, use_global_device_ids=true, to_apply=%region_10.11 | all-reduce | flops 513 | bytes 4104 | tf_op jit(solution)/shard_map/psum | solution.py:36
  80.4 1.4 fusion.15
  81.8 0.0 reduce-scatter.3.cloned.1.call-update
  81.8 0.0 all-reduce.7.cloned.1.call-start
  81.9 79.8 %all-reduce.5.cloned.1.call-done = f32[256,256]{1,0:T(8,128)} async-done(((f32[256,256]{1,0:T(8,128)}), f32[256,256]{1,0:T(8,128)}) %all-reduce.5.cloned.1.call-update) | async-done | bytes 262160 | tf_op jit(solution)/shard_map/psum | solution.py:54
  161.7 1.6 multiply_reduce_fusion.3
  164.0 0.0 reduce-scatter.3.cloned.1.call-done
  164.0 1.2 fusion.29
  165.2 0.1 collective-permute-start.7
  165.3 5.1 %collective-permute-done.7 = bf16[64,256]{1,0:T(8,128)(2,1)S(1)} collective-permute-done((bf16[64,256]{1,0:T(8,128)(2,1)S(1)}, bf16[64,256]{1,0:T(8,128)(2,1)S(1)}, u32[]{:S(2)}, u32[]{:S(2)}) %collective-permute-start.7) | collective-permute-done | bytes 32800 | tf_op jit(solution)/shard_map/ppermute | solution.py:15
  170.4 0.0 collective-permute-start.8
  170.4 5.1 %collective-permute-done.8 = bf16[64,256]{1,0:T(8,128)(2,1)S(1)} collective-permute-done((bf16[64,256]{1,0:T(8,128)(2,1)S(1)}, bf16[64,256]{1,0:T(8,128)(2,1)S(1)}, u32[]{:S(2)}, u32[]{:S(2)}) %collective-permute-start.8) | collective-permute-done | bytes 32800 | tf_op jit(solution)/shard_map/ppermute | solution.py:15
  175.6 0.0 collective-permute-start.9
  175.6 5.1 %collective-permute-done.9 = bf16[64,256]{1,0:T(8,128)(2,1)S(1)} collective-permute-done((bf16[64,256]{1,0:T(8,128)(2,1)S(1)}, bf16[64,256]{1,0:T(8,128)(2,1)S(1)}, u32[]{:S(2)}, u32[]{:S(2)}) %collective-permute-start.9) | collective-permute-done | bytes 32800 | tf_op jit(solution)/shard_map/ppermute | solution.py:15
  180.7 0.0 collective-permute-start.10
  180.7 5.1 %collective-permute-done.10 = bf16[64,256]{1,0:T(8,128)(2,1)S(1)} collective-permute-done((bf16[64,256]{1,0:T(8,128)(2,1)S(1)}, bf16[64,256]{1,0:T(8,128)(2,1)S(1)}, u32[]{:S(2)}, u32[]{:S(2)}) %collective-permute-start.10) | collective-permute-done | bytes 32800 | tf_op jit(solution)/shard_map/ppermute | solution.py:15
  185.9 0.0 collective-permute-start.11
  185.9 5.1 %collective-permute-done.11 = bf16[64,256]{1,0:T(8,128)(2,1)S(1)} collective-permute-done((bf16[64,256]{1,0:T(8,128)(2,1)S(1)}, bf16[64,256]{1,0:T(8,128)(2,1)S(1)}, u32[]{:S(2)}, u32[]{:S(2)}) %collective-permute-start.11) | collective-permute-done | bytes 32800 | tf_op jit(solution)/shard_map/ppermute | solution.py:15
  191.0 0.0 collective-permute-start.12
  191.0 5.1 %collective-permute-done.12 = bf16[64,256]{1,0:T(8,128)(2,1)S(1)} collective-permute-done((bf16[64,256]{1,0:T(8,128)(2,1)S(1)}, bf16[64,256]{1,0:T(8,128)(2,1)S(1)}, u32[]{:S(2)}, u32[]{:S(2)}) %collective-permute-start.12) | collective-permute-done | bytes 32800 | tf_op jit(solution)/shard_map/ppermute | solution.py:15
  196.1 0.0 collective-permute-start.13
  196.1 1.1 fusion.30
  197.3 0.0 all-reduce.7.cloned.1.call-update
  197.3 0.0 reduce-scatter.5.cloned.1.call-start
  197.3 3.9 %collective-permute-done.13 = bf16[64,256]{1,0:T(8,128)(2,1)S(1)} collective-permute-done((bf16[64,256]{1,0:T(8,128)(2,1)S(1)}, bf16[64,256]{1,0:T(8,128)(2,1)S(1)}, u32[]{:S(2)}, u32[]{:S(2)}) %collective-permute-start.13) | collective-permute-done | bytes 32800 | tf_op jit(solution)/shard_map/ppermute | solution.py:15
  201.3 1.4 fusion.12
  202.7 0.0 reduce-scatter.5.cloned.1.call-update
  202.7 121.7 %all-reduce.7.cloned.1.call-done = f32[256,256]{1,0:T(8,128)} async-done(((f32[256,256]{1,0:T(8,128)}), f32[256,256]{1,0:T(8,128)}) %all-reduce.7.cloned.1.call-update) | async-done | bytes 262160 | tf_op jit(solution)/shard_map/psum | solution.py:54
  324.5 1.6 multiply_reduce_fusion.2
  326.8 0.0 reduce-scatter.5.cloned.1.call-done
  326.8 1.8 fusion.7
  (18 shorter events, 0.1 us)
Async XLA Ops:
  7.4 45.8 %all-gather.2.cloned.1.call-start = ((), (), s32[]{:S(2)}) async-start(), calls=%async_computation.3 | async-start | bytes 1179648 | tf_op jit(solution)/shard_map/all_gather | solution.py:28
  8.1 153.6 %all-reduce.5.cloned.1.call-start = ((), (), s32[]{:S(2)}) async-start(), calls=%async_computation.2 | async-start | bytes 524288 | tf_op jit(solution)/shard_map/psum | solution.py:54
  9.0 6.1 %collective-permute-start = (bf16[64,256]{1,0:T(8,128)(2,1)S(1)}, bf16[64,256]{1,0:T(8,128)(2,1)S(1)}, u32[]{:S(2)}, u32[]{:S(2)}) collective-permute-start(bf16[64,256]{1,0:T(8,128)(2,1)S(1)} %multiply_convert_fusion), channel_id=1, source_target_pairs={{0,4},{4,8},{8,12},{12,16},{16,20},{20,24},{24,28},{28,0},{1,5},{5... | collective-permute-start | bytes 98312 | tf_op jit(solution)/shard_map/ppermute | solution.py:15
  15.1 5.1 %collective-permute-start.1 = (bf16[64,256]{1,0:T(8,128)(2,1)S(1)}, bf16[64,256]{1,0:T(8,128)(2,1)S(1)}, u32[]{:S(2)}, u32[]{:S(2)}) collective-permute-start(bf16[64,256]{1,0:T(8,128)(2,1)S(1)} %collective-permute-done), channel_id=1, source_target_pairs={{0,4},{4,8},{8,12},{12,16},{16,20},{20,24},{24,28},{28,0},{1,5},{5... | collective-permute-start | bytes 98312 | tf_op jit(solution)/shard_map/ppermute | solution.py:15
  20.2 5.6 %collective-permute-start.2 = (bf16[64,256]{1,0:T(8,128)(2,1)S(1)}, bf16[64,256]{1,0:T(8,128)(2,1)S(1)}, u32[]{:S(2)}, u32[]{:S(2)}) collective-permute-start(bf16[64,256]{1,0:T(8,128)(2,1)S(1)} %collective-permute-done.1), channel_id=1, source_target_pairs={{0,4},{4,8},{8,12},{12,16},{16,20},{20,24},{24,28},{28,0},{1,5},{5... | collective-permute-start | bytes 98312 | tf_op jit(solution)/shard_map/ppermute | solution.py:15
  25.8 5.8 %collective-permute-start.3 = (bf16[64,256]{1,0:T(8,128)(2,1)S(1)}, bf16[64,256]{1,0:T(8,128)(2,1)S(1)}, u32[]{:S(2)}, u32[]{:S(2)}) collective-permute-start(bf16[64,256]{1,0:T(8,128)(2,1)S(1)} %collective-permute-done.2), channel_id=1, source_target_pairs={{0,4},{4,8},{8,12},{12,16},{16,20},{20,24},{24,28},{28,0},{1,5},{5... | collective-permute-start | bytes 98312 | tf_op jit(solution)/shard_map/ppermute | solution.py:15
  31.6 5.1 %collective-permute-start.4 = (bf16[64,256]{1,0:T(8,128)(2,1)S(1)}, bf16[64,256]{1,0:T(8,128)(2,1)S(1)}, u32[]{:S(2)}, u32[]{:S(2)}) collective-permute-start(bf16[64,256]{1,0:T(8,128)(2,1)S(1)} %collective-permute-done.3), channel_id=1, source_target_pairs={{0,4},{4,8},{8,12},{12,16},{16,20},{20,24},{24,28},{28,0},{1,5},{5... | collective-permute-start | bytes 98312 | tf_op jit(solution)/shard_map/ppermute | solution.py:15
  33.7 19.5 %copy-start = (f32[64,256]{1,0:T(8,128)S(1)}, f32[64,256]{1,0:T(8,128)}, u32[]{:S(2)}) copy-start(f32[64,256]{1,0:T(8,128)} %param.5) | copy-start | bytes 196612
  33.7 130.3 %reduce-scatter.3.cloned.1.call-start = ((), (), s32[]{:S(2)}) async-start(), calls=%async_computation.4 | async-start | bytes 327680 | tf_op jit(solution)/shard_map/reduce_scatter | solution.py:45
  36.8 11.1 %collective-permute-start.5 = (bf16[64,256]{1,0:T(8,128)(2,1)S(1)}, bf16[64,256]{1,0:T(8,128)(2,1)S(1)}, u32[]{:S(2)}, u32[]{:S(2)}) collective-permute-start(bf16[64,256]{1,0:T(8,128)(2,1)S(1)} %collective-permute-done.4), channel_id=1, source_target_pairs={{0,4},{4,8},{8,12},{12,16},{16,20},{20,24},{24,28},{28,0},{1,5},{5... | collective-permute-start | bytes 98312 | tf_op jit(solution)/shard_map/ppermute | solution.py:15
  47.8 5.2 %collective-permute-start.6 = (bf16[64,256]{1,0:T(8,128)(2,1)S(1)}, bf16[64,256]{1,0:T(8,128)(2,1)S(1)}, u32[]{:S(2)}, u32[]{:S(2)}) collective-permute-start(bf16[64,256]{1,0:T(8,128)(2,1)S(1)} %collective-permute-done.5), channel_id=1, source_target_pairs={{0,4},{4,8},{8,12},{12,16},{16,20},{20,24},{24,28},{28,0},{1,5},{5... | collective-permute-start | bytes 98312 | tf_op jit(solution)/shard_map/ppermute | solution.py:15
  53.2 1.6 copy-start.1
  81.8 242.7 %all-reduce.7.cloned.1.call-start = ((), (), s32[]{:S(2)}) async-start(), calls=%async_computation.5 | async-start | bytes 524288 | tf_op jit(solution)/shard_map/psum | solution.py:54
  165.2 5.2 %collective-permute-start.7 = (bf16[64,256]{1,0:T(8,128)(2,1)S(1)}, bf16[64,256]{1,0:T(8,128)(2,1)S(1)}, u32[]{:S(2)}, u32[]{:S(2)}) collective-permute-start(bf16[64,256]{1,0:T(8,128)(2,1)S(1)} %get-tuple-element.14), channel_id=1, source_target_pairs={{0,4},{4,8},{8,12},{12,16},{16,20},{20,24},{24,28},{28,0},{1,5},{5... | collective-permute-start | bytes 98312 | tf_op jit(solution)/shard_map/ppermute | solution.py:15
  170.4 5.1 %collective-permute-start.8 = (bf16[64,256]{1,0:T(8,128)(2,1)S(1)}, bf16[64,256]{1,0:T(8,128)(2,1)S(1)}, u32[]{:S(2)}, u32[]{:S(2)}) collective-permute-start(bf16[64,256]{1,0:T(8,128)(2,1)S(1)} %collective-permute-done.7), channel_id=1, source_target_pairs={{0,4},{4,8},{8,12},{12,16},{16,20},{20,24},{24,28},{28,0},{1,5},{5... | collective-permute-start | bytes 98312 | tf_op jit(solution)/shard_map/ppermute | solution.py:15
  175.6 5.1 %collective-permute-start.9 = (bf16[64,256]{1,0:T(8,128)(2,1)S(1)}, bf16[64,256]{1,0:T(8,128)(2,1)S(1)}, u32[]{:S(2)}, u32[]{:S(2)}) collective-permute-start(bf16[64,256]{1,0:T(8,128)(2,1)S(1)} %collective-permute-done.8), channel_id=1, source_target_pairs={{0,4},{4,8},{8,12},{12,16},{16,20},{20,24},{24,28},{28,0},{1,5},{5... | collective-permute-start | bytes 98312 | tf_op jit(solution)/shard_map/ppermute | solution.py:15
  180.7 5.1 %collective-permute-start.10 = (bf16[64,256]{1,0:T(8,128)(2,1)S(1)}, bf16[64,256]{1,0:T(8,128)(2,1)S(1)}, u32[]{:S(2)}, u32[]{:S(2)}) collective-permute-start(bf16[64,256]{1,0:T(8,128)(2,1)S(1)} %collective-permute-done.9), channel_id=1, source_target_pairs={{0,4},{4,8},{8,12},{12,16},{16,20},{20,24},{24,28},{28,0},{1,5},{5... | collective-permute-start | bytes 98312 | tf_op jit(solution)/shard_map/ppermute | solution.py:15
  185.9 5.1 %collective-permute-start.11 = (bf16[64,256]{1,0:T(8,128)(2,1)S(1)}, bf16[64,256]{1,0:T(8,128)(2,1)S(1)}, u32[]{:S(2)}, u32[]{:S(2)}) collective-permute-start(bf16[64,256]{1,0:T(8,128)(2,1)S(1)} %collective-permute-done.10), channel_id=1, source_target_pairs={{0,4},{4,8},{8,12},{12,16},{16,20},{20,24},{24,28},{28,0},{1,5},{5... | collective-permute-start | bytes 98312 | tf_op jit(solution)/shard_map/ppermute | solution.py:15
  191.0 5.1 %collective-permute-start.12 = (bf16[64,256]{1,0:T(8,128)(2,1)S(1)}, bf16[64,256]{1,0:T(8,128)(2,1)S(1)}, u32[]{:S(2)}, u32[]{:S(2)}) collective-permute-start(bf16[64,256]{1,0:T(8,128)(2,1)S(1)} %collective-permute-done.11), channel_id=1, source_target_pairs={{0,4},{4,8},{8,12},{12,16},{16,20},{20,24},{24,28},{28,0},{1,5},{5... | collective-permute-start | bytes 98312 | tf_op jit(solution)/shard_map/ppermute | solution.py:15
  196.1 5.1 %collective-permute-start.13 = (bf16[64,256]{1,0:T(8,128)(2,1)S(1)}, bf16[64,256]{1,0:T(8,128)(2,1)S(1)}, u32[]{:S(2)}, u32[]{:S(2)}) collective-permute-start(bf16[64,256]{1,0:T(8,128)(2,1)S(1)} %collective-permute-done.12), channel_id=1, source_target_pairs={{0,4},{4,8},{8,12},{12,16},{16,20},{20,24},{24,28},{28,0},{1,5},{5... | collective-permute-start | bytes 98312 | tf_op jit(solution)/shard_map/ppermute | solution.py:15
  197.3 129.5 %reduce-scatter.5.cloned.1.call-start = ((), (), s32[]{:S(2)}) async-start(), calls=%async_computation.6 | async-start | bytes 327680 | tf_op jit(solution)/shard_map/reduce_scatter | solution.py:45
Sparse Core Ops, SparseCore 0:
  9.8 24.9 all-gather.1
  81.9 21.3 reduce-scatter.2
  202.9 23.4 reduce-scatter.4
Sparse Core Ops, SparseCore 1:
  33.8 127.9 all-reduce.4
  197.4 127.1 all-reduce.6
